TPU v7x, 32 devices: a whole 2x2x4 slice. The times are simulated.
32 devices in a mesh: day: 2 (over y), stu: 16 (over z, x, core).
Axes of the slice: x: 2, y: 2, z: 4, core: 2. Of those that a mesh axis runs over, the one named last changes fastest.
Arguments:
- performance: bfloat16 [64, 128, 1024], P('day', 'stu'), may hold values from -8 to 8
- student_factor: bfloat16 [128, 256], P('stu'), may hold values from -0.5 to 0.5
- skill_factor: bfloat16 [1024, 256], replicated, may hold values from -0.1875 to 0.1875
- day_prev: float32 [64, 256], P('day'), may hold values from -6 to 6
- ar_coef: float32 [7], replicated, may hold values from -0.3 to 0.3
Outputs:
- day_factor: float32 [64, 256], P('day', 'stu')
- residual: float32 [64, 256], P('day', 'stu')
All inputs are finite; a program needn't handle non-finite values.
Results may differ from a plain program's by a relative error of at most 0.0003.
Values sent between devices are 32-bit elements; how exact they have to be, the bound alone decides.
No kernel may reach another device: no remote copies, remote signals or barrier semaphores. Data moves between devices by JAX's collectives and lax.ppermute only.
A program may use at most 64 MiB of HBM per device.

v0:
```python
import jax
import jax.numpy as jnp
from jax import lax
from jax.sharding import PartitionSpec as P

LAGS = 7
ITERS = 3
smoothing = 1.0


def shifted(block, axis, distance):
    devices = range(lax.axis_size(axis))
    route = [(i - distance, i) for i in devices if i - distance in devices]
    return lax.ppermute(block, axis, route)


def filter_rows(extended, coef, count):
    out = extended[LAGS : LAGS + count]
    for lag in range(1, LAGS + 1):
        out = out - coef[lag - 1] * extended[LAGS - lag : LAGS - lag + count]
    return out


def smooth(values, coef):
    count = values.shape[0]
    below = shifted(values[count - LAGS :], "day", 1)
    ahead_core = filter_rows(jnp.concatenate([below, values], 0), coef, count)
    above = shifted(ahead_core[:LAGS], "day", -1)
    ahead = jnp.concatenate([ahead_core, above], 0)
    out = ahead[:count]
    for lag in range(1, LAGS + 1):
        out = out - coef[lag - 1] * ahead[lag : lag + count]
    return out


def with_gram(values, gram_part):
    return jnp.dot(
        lax.all_gather(values, "stu", axis=1, tiled=True),
        gram_part,
        precision=lax.Precision.HIGHEST,
        preferred_element_type=jnp.float32,
    )


def operate(values, gram_part, coef):
    return with_gram(values, gram_part) + smoothing * smooth(values, coef)


def global_total(value):
    return lax.psum(value, ("day", "stu"))


def summed_gram(local_gram):
    return lax.psum(local_gram, "stu")


def local(performance, student_factor, skill_factor, day_prev, ar_coef):
    days, students, skills = performance.shape
    rank = skill_factor.shape[1]
    proj = jnp.dot(
        performance.reshape(days * students, skills),
        skill_factor,
        preferred_element_type=jnp.float32,
    )
    proj = proj.reshape(days, students, rank)
    local_terms = jnp.sum(proj * student_factor.astype(jnp.float32)[None], axis=1)
    local_gram = jnp.dot(student_factor.T, student_factor, preferred_element_type=jnp.float32)
    skill_gram = jnp.dot(skill_factor.T, skill_factor, preferred_element_type=jnp.float32)
    columns = rank // lax.axis_size("stu")
    first_col = lax.axis_index("stu") * columns
    gram = summed_gram(local_gram) * skill_gram
    mttkrp = lax.psum_scatter(local_terms, "stu", scatter_dimension=1, tiled=True)
    gram_part = lax.dynamic_slice_in_dim(gram, first_col, columns, 1)
    day_factor = lax.dynamic_slice_in_dim(day_prev, first_col, columns, 1)
    residual = mttkrp - operate(day_factor, gram_part, ar_coef)
    direction = residual
    norm_now = global_total(jnp.sum(residual * residual))
    for step in range(ITERS):
        image = operate(direction, gram_part, ar_coef)
        alpha = norm_now / global_total(jnp.sum(direction * image))
        day_factor = day_factor + alpha * direction
        residual = residual - alpha * image
        norm_next = global_total(jnp.sum(residual * residual))
        direction = residual + norm_next / norm_now * direction
        norm_now = norm_next
    return (day_factor, residual)


def solution(mesh):
    return jax.shard_map(
        local,
        mesh=mesh,
        in_specs=(P("day", "stu", None), P("stu", None), P(), P("day", None), P()),
        out_specs=(P("day", "stu"), P("day", "stu")),
        check_vma=False,
    )
```

profile of v0, /device:TPU:14, one launch (start us, length us, event | category | flops | bytes accessed | tf_op | source)
XLA Modules:
  0.0 491.8 jit_solution(908321572501885240)
XLA Ops:
  7.2 0.0 copy-start
  7.2 0.0 copy-start.1
  7.2 0.0 all-reduce.3.cloned.1.call-start
  7.2 0.9 constant_dynamic-slice_fusion
  8.1 0.1 copy.10
  8.2 0.1 slice.333
  8.3 1.3 collective-permute-start
  9.6 1.7 fusion.139
  11.2 0.0 copy-start.2
  11.2 0.0 all-reduce.3.cloned.1.call-update
  11.3 0.0 reduce-scatter.2.cloned.1.call-start
  11.3 0.6 copy-done.2
  11.9 0.0 copy-done
  11.9 0.0 copy-done.1
  11.9 0.3 fusion
  12.3 0.8 copy.9
  13.0 0.0 reduce-scatter.2.cloned.1.call-update
  13.0 0.0 copy-start.3
  13.1 0.3 fusion.140
  13.4 0.3 copy-done.3
  13.7 0.7 fusion.138
  14.3 15.5 %all_gather.12 = f32[32,256]{0,1:T(8,128)S(1)} all-gather(f32[32,16]{0,1:T(8,128)S(1)} %copy.10), channel_id=1, replica_groups=mesh['day'=2,'stu'=16] {'stu'}, dimensions={1}, use_global_device_ids=true | all-gather | bytes 34816 | tf_op jit(solution)/shard_map/all_gather | solution.py:38
  29.8 0.0 collective-permute-done
  29.8 4.5 fusion.120
  34.3 4.6 collective-permute-start.1
  38.9 64.2 %all-reduce.3.cloned.1.call-done = f32[256,256]{0,1:T(8,128)} async-done(((f32[256,256]{0,1:T(8,128)}), f32[256,256]{0,1:T(8,128)}) %all-reduce.3.cloned.1.call-update) | async-done | bytes 262160 | tf_op jit(solution)/shard_map/psum | solution.py:54
  103.1 0.7 dynamic-slice_multiply_fusion
  103.8 0.0 collective-permute-done.1
  103.8 57.7 %reduce-scatter.2.cloned.1.call-done = f32[32,16]{0,1:T(8,128)} async-done(((f32[32,256]{0,1:T(8,128)}), f32[32,16]{0,1:T(8,128)}) %reduce-scatter.2.cloned.1.call-update) | async-done | bytes 2064 | tf_op jit(solution)/shard_map/reduce_scatter | solution.py:72
  161.5 5.2 %fusion.104 = f32[32,16]{0,1:T(8,128)S(1)} fusion(f32[32,16]{0,1:T(8,128)} %reduce-scatter.2.cloned.1.call-done, f32[7,16]{0,1:T(8,128)S(1)} %collective-permute-done.1, f32[32,16]{0,1:T(8,128)S(1)} %fusion.120, f32[]{:T(128)} %bitcast.7, f32[]{:T(128)} %bitcast.6, f32[]{:T(128)} %bitcast.5, f32[]{:T(128)} %bitcast.4, f32[]{:T(128)} %bitcast.3, ...), kind=kOutput, calls=%fused_computation.173 | convolution fusion | flops 1584640 | bytes 55772 | tf_op jit(solution)/shard_map/dot_general | solution.py:37
  166.7 0.1 slice.359
  166.8 1.3 collective-permute-start.2
  168.1 4.2 collective-permute-done.2
  172.3 4.5 fusion.86
  176.8 1.6 collective-permute-start.3
  178.5 15.4 %all_gather.13 = f32[32,256]{0,1:T(8,128)S(1)} all-gather(f32[32,16]{0,1:T(8,128)S(1)} %fusion.104), channel_id=1, replica_groups=mesh['day'=2,'stu'=16] {'stu'}, dimensions={1}, use_global_device_ids=true | all-gather | bytes 34816 | tf_op jit(solution)/shard_map/all_gather | solution.py:38
  193.8 0.0 collective-permute-done.3
  193.8 5.2 %multiply_reduce_fusion.4 = (f32[]{:T(128)}, f32[]{:T(128)}, f32[32,16]{0,1:T(8,128)S(1)}) fusion(f32[32,16]{0,1:T(8,128)S(1)} %fusion.104, f32[7,16]{0,1:T(8,128)S(1)} %collective-permute-done.3, f32[32,16]{0,1:T(8,128)S(1)} %fusion.86, f32[]{:T(128)} %bitcast.7, f32[]{:T(128)} %bitcast.6, f32[]{:T(128)} %bitcast.5, f32[]{:T(128)} %bitcast.4, ...), kind=kOutput, calls=%fused_computation.235 | convolution fusion | flops 1586174 | bytes 55780 | tf_op jit(solution)/shard_map/dot_general | solution.py:37
  199.0 44.1 %all-reduce = (f32[]{:T(128)}, f32[]{:T(128)}) all-reduce(f32[]{:T(128)} %get-tuple-element.3, f32[]{:T(128)} %get-tuple-element.2), channel_id=1, replica_groups=mesh['day'=2,'stu'=16] {'day','stu'}, use_global_device_ids=true, to_apply=%region_4.0 | all-reduce | flops 2 | bytes 16 | tf_op jit(solution)/shard_map/psum | solution.py:50
  244.4 0.6 multiply_reduce_fusion.3
  245.1 38.6 %psum.52 = f32[]{:T(128)} all-reduce(f32[]{:T(128)} %multiply_reduce_fusion.3), channel_id=1, replica_groups=mesh['day'=2,'stu'=16] {'day','stu'}, use_global_device_ids=true, to_apply=%region_8.0 | all-reduce | flops 1 | bytes 8 | tf_op jit(solution)/shard_map/psum | solution.py:50
  285.1 0.1 slice.385
  285.1 1.3 collective-permute-start.4
  286.4 4.2 collective-permute-done.4
  290.7 4.5 fusion.53
  295.1 1.6 collective-permute-start.5
  296.8 18.0 %all_gather.14 = f32[32,256]{0,1:T(8,128)S(1)} all-gather(f32[32,16]{0,1:T(8,128)S(1)} %multiply_add_fusion.2), channel_id=1, replica_groups=mesh['day'=2,'stu'=16] {'stu'}, dimensions={1}, use_global_device_ids=true | all-gather | bytes 34816 | tf_op jit(solution)/shard_map/all_gather | solution.py:38
  314.8 0.0 collective-permute-done.5
  314.8 5.2 %multiply_reduce_fusion.2 = (f32[]{:T(128)}, f32[32,16]{0,1:T(8,128)S(1)}) fusion(f32[32,16]{0,1:T(8,128)S(1)} %multiply_add_fusion.2, f32[7,16]{0,1:T(8,128)S(1)} %collective-permute-done.5, f32[32,16]{0,1:T(8,128)S(1)} %fusion.53, f32[]{:T(128)} %bitcast.7, f32[]{:T(128)} %bitcast.6, f32[]{:T(128)} %bitcast.5, f32[]{:T(128)} %bitcast.4, f32[]{:T(128)} %bitcast.3, ...), kind=kOutput, calls=%fused_computation.231 | convolution fusion | flops 1585151 | bytes 55776 | tf_op jit(solution)/shard_map/dot_general | solution.py:37
  320.0 43.0 %psum.53 = f32[]{:T(128)} all-reduce(f32[]{:T(128)} %get-tuple-element.10), channel_id=1, replica_groups=mesh['day'=2,'stu'=16] {'day','stu'}, use_global_device_ids=true, to_apply=%region_10.0 | all-reduce | flops 1 | bytes 8 | tf_op jit(solution)/shard_map/psum | solution.py:50
  364.2 0.6 multiply_reduce_fusion.1
  364.8 39.0 %psum.54 = f32[]{:T(128)} all-reduce(f32[]{:T(128)} %get-tuple-element.8), channel_id=1, replica_groups=mesh['day'=2,'stu'=16] {'day','stu'}, use_global_device_ids=true, to_apply=%region_12.0 | all-reduce | flops 1 | bytes 8 | tf_op jit(solution)/shard_map/psum | solution.py:50
  405.2 0.1 slice.411
  405.3 1.3 collective-permute-start.6
  406.5 4.2 collective-permute-done.6
  410.8 4.5 fusion.20
  415.3 1.6 collective-permute-start.7
  416.9 17.6 %all_gather.15 = f32[32,256]{0,1:T(8,128)S(1)} all-gather(f32[32,16]{0,1:T(8,128)S(1)} %multiply_add_fusion.1), channel_id=1, replica_groups=mesh['day'=2,'stu'=16] {'stu'}, dimensions={1}, use_global_device_ids=true | all-gather | bytes 34816 | tf_op jit(solution)/shard_map/all_gather | solution.py:38
  434.5 0.0 collective-permute-done.7
  434.5 5.1 %multiply_reduce_fusion = (f32[]{:T(128)}, f32[32,16]{0,1:T(8,128)S(1)}) fusion(f32[32,16]{0,1:T(8,128)S(1)} %multiply_add_fusion.1, f32[7,16]{0,1:T(8,128)S(1)} %collective-permute-done.7, f32[32,16]{0,1:T(8,128)S(1)} %fusion.20, f32[]{:T(128)} %bitcast.7, f32[]{:T(128)} %bitcast.6, f32[]{:T(128)} %bitcast.5, f32[]{:T(128)} %bitcast.4, f32[]{:T(128)} %bitcast.3, ...), kind=kOutput, calls=%fused_computation.227 | convolution fusion | flops 1585151 | bytes 55776 | tf_op jit(solution)/shard_map/dot_general | solution.py:37
  439.7 43.2 %psum.55 = f32[]{:T(128)} all-reduce(f32[]{:T(128)} %get-tuple-element.6), channel_id=1, replica_groups=mesh['day'=2,'stu'=16] {'day','stu'}, use_global_device_ids=true, to_apply=%region_14.0 | all-reduce | flops 1 | bytes 8 | tf_op jit(solution)/shard_map/psum | solution.py:50
  484.3 0.6 multiply_subtract_fusion
  (3 shorter events, 0.0 us)
Async XLA Ops:
  7.2 4.8 copy-start
  7.2 4.8 copy-start.1
  7.2 95.9 %all-reduce.3.cloned.1.call-start = ((), (), s32[]{:S(2)}) async-start(), calls=%async_computation.2 | async-start | bytes 524288 | tf_op jit(solution)/shard_map/psum | solution.py:54
  8.3 21.6 %collective-permute-start = (f32[7,16]{0,1:T(8,128)S(1)}, f32[7,16]{0,1:T(8,128)S(1)}, u32[]{:S(2)}, u32[]{:S(2)}) collective-permute-start(f32[7,16]{0,1:T(8,128)S(1)} %slice.333), channel_id=1, source_target_pairs={{0,16},{1,17},{2,18},{3,19},{4,20},{5,21},{6,22},{7,23},{8,24},{9,... | collective-permute-start | bytes 1352 | tf_op jit(solution)/shard_map/ppermute | solution.py:14
  11.2 0.7 copy-start.2
  11.3 150.2 %reduce-scatter.2.cloned.1.call-start = ((), (), s32[]{:S(2)}) async-start(), calls=%async_computation.1 | async-start | bytes 139264 | tf_op jit(solution)/shard_map/reduce_scatter | solution.py:72
  13.0 0.7 copy-start.3
  34.3 69.5 %collective-permute-start.1 = (f32[7,16]{0,1:T(8,128)S(1)}, f32[7,16]{0,1:T(8,128)S(1)}, u32[]{:S(2)}, u32[]{:S(2)}) collective-permute-start(f32[7,16]{0,1:T(8,128)S(1)} %bitcast.27), channel_id=1, source_target_pairs={{16,0},{17,1},{18,2},{19,3},{20,4},{21,5},{22,6},{23,7},{24,8},{25... | collective-permute-start | bytes 1352 | tf_op jit(solution)/shard_map/ppermute | solution.py:14
  166.8 5.5 %collective-permute-start.2 = (f32[7,16]{0,1:T(8,128)S(1)}, f32[7,16]{0,1:T(8,128)S(1)}, u32[]{:S(2)}, u32[]{:S(2)}) collective-permute-start(f32[7,16]{0,1:T(8,128)S(1)} %slice.359), channel_id=1, source_target_pairs={{0,16},{1,17},{2,18},{3,19},{4,20},{5,21},{6,22},{7,23},{8,24},{9,... | collective-permute-start | bytes 1352 | tf_op jit(solution)/shard_map/ppermute | solution.py:14
  176.8 17.0 %collective-permute-start.3 = (f32[7,16]{0,1:T(8,128)S(1)}, f32[7,16]{0,1:T(8,128)S(1)}, u32[]{:S(2)}, u32[]{:S(2)}) collective-permute-start(f32[7,16]{0,1:T(8,128)S(1)} %bitcast.29), channel_id=1, source_target_pairs={{16,0},{17,1},{18,2},{19,3},{20,4},{21,5},{22,6},{23,7},{24,8},{25... | collective-permute-start | bytes 1352 | tf_op jit(solution)/shard_map/ppermute | solution.py:14
  285.1 5.5 %collective-permute-start.4 = (f32[7,16]{0,1:T(8,128)S(1)}, f32[7,16]{0,1:T(8,128)S(1)}, u32[]{:S(2)}, u32[]{:S(2)}) collective-permute-start(f32[7,16]{0,1:T(8,128)S(1)} %slice.385), channel_id=1, source_target_pairs={{0,16},{1,17},{2,18},{3,19},{4,20},{5,21},{6,22},{7,23},{8,24},{9,... | collective-permute-start | bytes 1352 | tf_op jit(solution)/shard_map/ppermute | solution.py:14
  295.1 19.6 %collective-permute-start.5 = (f32[7,16]{0,1:T(8,128)S(1)}, f32[7,16]{0,1:T(8,128)S(1)}, u32[]{:S(2)}, u32[]{:S(2)}) collective-permute-start(f32[7,16]{0,1:T(8,128)S(1)} %bitcast.30), channel_id=1, source_target_pairs={{16,0},{17,1},{18,2},{19,3},{20,4},{21,5},{22,6},{23,7},{24,8},{25... | collective-permute-start | bytes 1352 | tf_op jit(solution)/shard_map/ppermute | solution.py:14
  405.3 5.5 %collective-permute-start.6 = (f32[7,16]{0,1:T(8,128)S(1)}, f32[7,16]{0,1:T(8,128)S(1)}, u32[]{:S(2)}, u32[]{:S(2)}) collective-permute-start(f32[7,16]{0,1:T(8,128)S(1)} %slice.411), channel_id=1, source_target_pairs={{0,16},{1,17},{2,18},{3,19},{4,20},{5,21},{6,22},{7,23},{8,24},{9,... | collective-permute-start | bytes 1352 | tf_op jit(solution)/shard_map/ppermute | solution.py:14
  415.3 19.3 %collective-permute-start.7 = (f32[7,16]{0,1:T(8,128)S(1)}, f32[7,16]{0,1:T(8,128)S(1)}, u32[]{:S(2)}, u32[]{:S(2)}) collective-permute-start(f32[7,16]{0,1:T(8,128)S(1)} %bitcast.28), channel_id=1, source_target_pairs={{16,0},{17,1},{18,2},{19,3},{20,4},{21,5},{22,6},{23,7},{24,8},{25... | collective-permute-start | bytes 1352 | tf_op jit(solution)/shard_map/ppermute | solution.py:14
Sparse Core Ops, SparseCore 0:
  11.4 91.6 all-reduce.2
  106.5 54.8 reduce-scatter.1
where the time goes:
time: 494 us; the launch traced here: 492 us
  blocking collectives  274 us (55%)
  waiting for transfers between devices  135 us (27%)
  matrix products  23.1 us (5%)
  between operations  20.9 us (4%)
  other arithmetic  20.4 us (4%)
  starting transfers between devices  14.7 us (3%)
    psum x5, blocking collectives, global_total(): return lax.psum(value, ('day', 'stu'))  208 us
    all_gather x4, blocking collectives, with_gram(): lax.all_gather(values, 'stu', axis=1, tiled=True)  66.5 us
    psum x1, waiting for transfers between devices, summed_gram(): return lax.psum(local_gram, 'stu')  64.2 us
    reduce_scatter x1, waiting for transfers between devices, local(): lax.psum_scatter(local_terms, 'stu', scatter_dimension=1, tiled=True)  57.7 us
    dot_general x4, matrix products, with_gram(): jnp.dot(lax.all_gather(values, 'stu', axis=1, tiled=True), gram_part, pre...  20.8 us
    sub x4, other arithmetic, filter_rows(): out = out - coef[lag - 1] * extended[LAGS - lag:LAGS - lag + count]  17.8 us
    ppermute x8, starting transfers between devices, shifted(): return lax.ppermute(block, axis, route)  14.6 us
    ppermute x8, waiting for transfers between devices, shifted(): return lax.ppermute(block, axis, route)  12.7 us
  transfers between devices with their start and end apart: 10, of which 5 were waited for; matrix products, arithmetic and copies ran while one was open for 2% of the time, Pallas kernels for 0%

commit v1 on v0

--- a/solution.py
+++ b/solution.py
@@ -1,11 +1,29 @@
+import functools
 import jax
 import jax.numpy as jnp
 from jax import lax
 from jax.sharding import PartitionSpec as P
+from jax.lax import axis_index, ppermute, psum
 
 LAGS = 7
 ITERS = 3
 smoothing = 1.0
+
+
+def create_sectors(in_array, mesh_name):
+    extent = psum(1, mesh_name)
+    queue = tuple(((num, (num + 1) % extent) for num in range(extent)))
+    steps_seen = tuple(((num, (num - 1) % extent) for num in range(extent)))
+    n_now, last = ([in_array], [in_array])
+    for _ in range(extent // 2):
+        n_now.append(ppermute(n_now[-1], mesh_name, queue))
+    for _ in tuple(range((extent - 1) // 2)):
+        last.append(ppermute(last[-1], mesh_name, steps_seen))
+    z = jnp.concatenate([*n_now[::-1], *last[1:]], 1)
+    return jnp.roll(z, (axis_index(mesh_name) - extent // 2) * in_array.shape[1], 1)
+
+
+masks_scan = functools.partial(create_sectors, mesh_name="stu")
 
 
 def shifted(block, axis, distance):
@@ -35,7 +53,7 @@
 
 def with_gram(values, gram_part):
     return jnp.dot(
-        lax.all_gather(values, "stu", axis=1, tiled=True),
+        masks_scan(values),
         gram_part,
         precision=lax.Precision.HIGHEST,
         preferred_element_type=jnp.float32,

time: 494 us -> 572 us (1.16)
  starting transfers between devices: 14.7 us -> 94.2 us
  blocking collectives: 274 us -> 245 us
  waiting for transfers between devices: 135 us -> 157 us
    ppermute x0 -> x60, starting transfers between devices: none -> 74.7 us  [the longest x32 48.2 us: create_sectors(): n_now.append(ppermute(n_now[-1], mesh_name, queue))]
    all_gather x4 -> x0, blocking collectives: 66.5 us -> none  [with_gram(): lax.all_gather(values, 'stu', axis=1, tiled=True)]
    psum x5, blocking collectives: 208 us -> 245 us  [global_total(): return lax.psum(value, ('day', 'stu'))]
    ppermute x0 -> x60, waiting for transfers between devices: none -> 23.5 us  [the longest x32 22.9 us: create_sectors(): n_now.append(ppermute(n_now[-1], mesh_name, queue))]
    ppermute x8, waiting for transfers between devices: 12.7 us -> 2.95 us  [shifted(): return lax.ppermute(block, axis, route)]
    psum x1, waiting for transfers between devices: 64.2 us -> 72.8 us  [summed_gram(): return lax.psum(local_gram, 'stu')]
  transfers between devices with their start and end apart: 10 -> 70, of which waited for: 5 -> 31; matrix products, arithmetic and copies ran while one was open for 2% -> 5% of each run, Pallas kernels for 0% -> 0%
where the time goes in v1:
time: 572 us; the launch traced here: 569 us
  blocking collectives  245 us (43%)
  waiting for transfers between devices  157 us (27%)
  starting transfers between devices  94.2 us (16%)
  matrix products  22.8 us (4%)
  between operations  21 us (4%)
  other arithmetic  20.6 us (4%)
  local copies, waits for them, and re-layouts  7.91 us (1%)
    psum x5, blocking collectives, global_total(): return lax.psum(value, ('day', 'stu'))  245 us
    psum x1, waiting for transfers between devices, summed_gram(): return lax.psum(local_gram, 'stu')  72.8 us
    reduce_scatter x1, waiting for transfers between devices, local(): lax.psum_scatter(local_terms, 'stu', scatter_dimension=1, tiled=True)  57.7 us
    ppermute x32, starting transfers between devices, create_sectors(): n_now.append(ppermute(n_now[-1], mesh_name, queue))  48.2 us
    ppermute x28, starting transfers between devices, create_sectors(): last.append(ppermute(last[-1], mesh_name, steps_seen))  26.5 us
    ppermute x32, waiting for transfers between devices, create_sectors(): n_now.append(ppermute(n_now[-1], mesh_name, queue))  22.9 us
    dot_general x4, matrix products, with_gram(): jnp.dot(masks_scan(values), gram_part, precision=lax.Precision.HIGHEST, p...  21.2 us
    ppermute x8, starting transfers between devices, shifted(): return lax.ppermute(block, axis, route)  19.5 us
  transfers between devices with their start and end apart: 70, of which 31 were waited for; matrix products, arithmetic and copies ran while one was open for 5% of the time, Pallas kernels for 0%

profile of v1, /device:TPU:14, one launch (start us, length us, event | category | flops | bytes accessed | tf_op | source)
XLA Modules:
  0.0 568.8 jit_solution(1478813211921856361)
XLA Ops:
  8.2 1.7 collective-permute-start.8
  9.9 1.3 collective-permute-done
  11.3 1.7 collective-permute-start.9
  13.0 1.3 collective-permute-done.1
  14.7 1.3 collective-permute-start.15
  16.0 1.5 collective-permute-start.10
  17.5 1.9 collective-permute-start.3
  20.6 2.7 collective-permute-start.4
  24.5 2.8 collective-permute-start.5
  28.1 3.1 collective-permute-start.6
  32.1 3.1 collective-permute-start.7
  35.2 4.5 fusion.142
  39.7 4.3 collective-permute-start.16
  45.3 72.8 %all-reduce.3.cloned.1.call-done = f32[256,256]{0,1:T(8,128)} async-done(((f32[256,256]{0,1:T(8,128)}), f32[256,256]{0,1:T(8,128)}) %all-reduce.3.cloned.1.call-update) | async-done | bytes 262160 | tf_op jit(solution)/shard_map/psum | solution.py:72
  118.8 57.7 %reduce-scatter.2.cloned.1.call-done = f32[32,16]{0,1:T(8,128)} async-done(((f32[32,256]{0,1:T(8,128)}), f32[32,16]{0,1:T(8,128)}) %reduce-scatter.2.cloned.1.call-update) | async-done | bytes 2064 | tf_op jit(solution)/shard_map/reduce_scatter | solution.py:90
  176.5 5.3 fusion.26
  181.9 1.7 collective-permute-start.25
  183.7 1.3 collective-permute-done.17
  185.0 1.7 collective-permute-start.26
  186.8 1.3 collective-permute-done.18
  188.1 2.0 collective-permute-start.27
  191.5 1.7 collective-permute-start.28
  194.2 1.2 collective-permute-start.21
  197.3 2.1 collective-permute-start.22
  199.4 1.1 collective-permute-done.22
  200.6 2.9 collective-permute-start.23
  203.5 1.3 collective-permute-start.32
  204.9 3.2 collective-permute-start.24
  209.0 4.5 fusion.110
  213.5 3.4 collective-permute-start.33
  218.2 5.3 multiply_reduce_fusion.4
  223.6 54.8 %all-reduce = (f32[]{:T(128)}, f32[]{:T(128)}) all-reduce(f32[]{:T(128)} %get-tuple-element.4, f32[]{:T(128)} %get-tuple-element.3), channel_id=1, replica_groups=mesh['day'=2,'stu'=16] {'day','stu'}, use_global_device_ids=true, to_apply=%region_4.6 | all-reduce | flops 2 | bytes 16 | tf_op jit(solution)/shard_map/psum | solution.py:68
  280.3 39.8 %psum.52 = f32[]{:T(128)} all-reduce(f32[]{:T(128)} %multiply_reduce_fusion.3), channel_id=1, replica_groups=mesh['day'=2,'stu'=16] {'day','stu'}, use_global_device_ids=true, to_apply=%region_8.10 | all-reduce | flops 1 | bytes 8 | tf_op jit(solution)/shard_map/psum | solution.py:68
  321.5 1.7 collective-permute-start.42
  323.3 1.3 collective-permute-done.34
  324.6 1.7 collective-permute-start.43
  326.3 1.3 collective-permute-done.35
  327.8 2.0 collective-permute-start.44
  331.8 1.0 collective-permute-start.45
  333.8 1.9 collective-permute-start.38
  336.9 2.8 collective-permute-start.39
  340.5 3.1 collective-permute-start.40
  343.8 1.3 collective-permute-start.49
  345.1 3.2 collective-permute-start.41
  349.3 4.5 fusion.78
  353.8 3.4 collective-permute-start.50
  358.5 5.3 multiply_reduce_fusion.2
  363.8 55.5 %psum.53 = f32[]{:T(128)} all-reduce(f32[]{:T(128)} %get-tuple-element.17), channel_id=1, replica_groups=mesh['day'=2,'stu'=16] {'day','stu'}, use_global_device_ids=true, to_apply=%region_10.12 | all-reduce | flops 1 | bytes 8 | tf_op jit(solution)/shard_map/psum | solution.py:68
  421.2 39.8 %psum.54 = f32[]{:T(128)} all-reduce(f32[]{:T(128)} %get-tuple-element.7), channel_id=1, replica_groups=mesh['day'=2,'stu'=16] {'day','stu'}, use_global_device_ids=true, to_apply=%region_12.14 | all-reduce | flops 1 | bytes 8 | tf_op jit(solution)/shard_map/psum | solution.py:68
  462.4 1.7 collective-permute-start.59
  464.1 1.3 collective-permute-done.51
  465.5 1.7 collective-permute-start.60
  467.2 1.3 collective-permute-done.52
  468.6 2.0 collective-permute-start.61
  472.6 1.0 collective-permute-start.62
  474.7 1.9 collective-permute-start.55
  477.8 2.8 collective-permute-start.56
  481.4 3.1 collective-permute-start.57
  484.6 1.3 collective-permute-start.66
  486.0 3.2 collective-permute-start.58
  490.2 4.5 fusion.46
  494.7 3.4 collective-permute-start.67
  499.4 5.3 multiply_reduce_fusion
  504.6 55.4 %psum.55 = f32[]{:T(128)} all-reduce(f32[]{:T(128)} %get-tuple-element.19), channel_id=1, replica_groups=mesh['day'=2,'stu'=16] {'day','stu'}, use_global_device_ids=true, to_apply=%region_14.16 | all-reduce | flops 1 | bytes 8 | tf_op jit(solution)/shard_map/psum | solution.py:68
  (184 shorter events, 31.3 us)
Async XLA Ops:
  7.2 110.9 %all-reduce.3.cloned.1.call-start = ((), (), s32[]{:S(2)}) async-start(), calls=%async_computation.2 | async-start | bytes 524288 | tf_op jit(solution)/shard_map/psum | solution.py:72
  8.2 3.1 collective-permute-start
  8.2 3.1 collective-permute-start.8
  11.3 3.1 collective-permute-start.1
  11.3 4.7 collective-permute-start.9
  14.3 3.2 collective-permute-start.2
  14.7 20.5 %collective-permute-start.15 = (f32[7,16]{0,1:T(8,128)S(1)}, f32[7,16]{0,1:T(8,128)S(1)}, u32[]{:S(2)}, u32[]{:S(2)}) collective-permute-start(f32[7,16]{0,1:T(8,128)S(1)} %slice.333), channel_id=1, source_target_pairs={{0,16},{1,17},{2,18},{3,19},{4,20},{5,21},{6,22},{7,23},{8,24},{9,... | collective-permute-start | bytes 1352 | tf_op jit(solution)/shard_map/ppermute | solution.py:32
  16.0 4.4 collective-permute-start.10
  17.5 3.1 collective-permute-start.3
  20.3 156.2 %reduce-scatter.2.cloned.1.call-start = ((), (), s32[]{:S(2)}) async-start(), calls=%async_computation.1 | async-start | bytes 139264 | tf_op jit(solution)/shard_map/reduce_scatter | solution.py:90
  20.4 4.0 collective-permute-start.11
  20.6 3.9 collective-permute-start.4
  24.4 3.5 collective-permute-start.12
  24.5 3.6 collective-permute-start.5
  27.9 4.0 collective-permute-start.13
  28.1 4.0 collective-permute-start.6
  31.9 13.1 %collective-permute-start.14 = (f32[32,16]{0,1:T(8,128)S(1)}, f32[32,16]{0,1:T(8,128)S(1)}, u32[]{:S(2)}, u32[]{:S(2)}) collective-permute-start(f32[32,16]{0,1:T(8,128)S(1)} %collective-permute-done.13), channel_id=1, source_target_pairs={{0,15},{1,0},{2,1},{3,2},{4,3},{5,4},{6,5},{7,6},{8,7},{9,8},{10,9... | collective-permute-start | bytes 6152 | tf_op jit(solution)/shard_map/ppermute | solution.py:21
  32.1 13.0 %collective-permute-start.7 = (f32[32,16]{0,1:T(8,128)S(1)}, f32[32,16]{0,1:T(8,128)S(1)}, u32[]{:S(2)}, u32[]{:S(2)}) collective-permute-start(f32[32,16]{0,1:T(8,128)S(1)} %collective-permute-done.6), channel_id=1, source_target_pairs={{0,1},{1,2},{2,3},{3,4},{4,5},{5,6},{6,7},{7,8},{8,9},{9,10},{10,1... | collective-permute-start | bytes 6152 | tf_op jit(solution)/shard_map/ppermute | solution.py:19
  39.7 79.1 %collective-permute-start.16 = (f32[7,16]{0,1:T(8,128)S(1)}, f32[7,16]{0,1:T(8,128)S(1)}, u32[]{:S(2)}, u32[]{:S(2)}) collective-permute-start(f32[7,16]{0,1:T(8,128)S(1)} %bitcast.23), channel_id=1, source_target_pairs={{16,0},{17,1},{18,2},{19,3},{20,4},{21,5},{22,6},{23,7},{24,8},{25... | collective-permute-start | bytes 1352 | tf_op jit(solution)/shard_map/ppermute | solution.py:32
  181.9 3.1 collective-permute-start.17
  181.9 3.1 collective-permute-start.25
  185.0 3.1 collective-permute-start.26
  188.1 3.4 collective-permute-start.27
  191.2 3.1 collective-permute-start.20
  191.5 4.0 collective-permute-start.28
  194.2 3.1 collective-permute-start.21
  195.5 4.0 collective-permute-start.29
  197.3 3.2 collective-permute-start.22
  199.4 5.4 collective-permute-start.30
  200.6 4.3 collective-permute-start.23
  203.5 5.5 collective-permute-start.32
  204.9 13.0 %collective-permute-start.31 = (f32[32,16]{0,1:T(8,128)S(1)}, f32[32,16]{0,1:T(8,128)S(1)}, u32[]{:S(2)}, u32[]{:S(2)}) collective-permute-start(f32[32,16]{0,1:T(8,128)S(1)} %collective-permute-done.30), channel_id=1, source_target_pairs={{0,15},{1,0},{2,1},{3,2},{4,3},{5,4},{6,5},{7,6},{8,7},{9,8},{10,9... | collective-permute-start | bytes 6152 | tf_op jit(solution)/shard_map/ppermute | solution.py:21
  204.9 13.1 %collective-permute-start.24 = (f32[32,16]{0,1:T(8,128)S(1)}, f32[32,16]{0,1:T(8,128)S(1)}, u32[]{:S(2)}, u32[]{:S(2)}) collective-permute-start(f32[32,16]{0,1:T(8,128)S(1)} %collective-permute-done.23), channel_id=1, source_target_pairs={{0,1},{1,2},{2,3},{3,4},{4,5},{5,6},{6,7},{7,8},{8,9},{9,10},{10,1... | collective-permute-start | bytes 6152 | tf_op jit(solution)/shard_map/ppermute | solution.py:19
  213.5 4.7 collective-permute-start.33
  321.5 3.1 collective-permute-start.34
  321.5 3.1 collective-permute-start.42
  324.6 3.1 collective-permute-start.35
  324.6 3.1 collective-permute-start.43
  327.7 3.1 collective-permute-start.36
  327.8 4.0 collective-permute-start.44
  330.7 3.1 collective-permute-start.37
  331.8 4.0 collective-permute-start.45
  333.8 3.1 collective-permute-start.38
  335.7 4.0 collective-permute-start.46
  336.9 3.6 collective-permute-start.39
  339.7 5.4 collective-permute-start.47
  340.5 4.6 collective-permute-start.40
  343.8 5.5 collective-permute-start.49
  345.1 13.0 %collective-permute-start.48 = (f32[32,16]{0,1:T(8,128)S(1)}, f32[32,16]{0,1:T(8,128)S(1)}, u32[]{:S(2)}, u32[]{:S(2)}) collective-permute-start(f32[32,16]{0,1:T(8,128)S(1)} %collective-permute-done.47), channel_id=1, source_target_pairs={{0,15},{1,0},{2,1},{3,2},{4,3},{5,4},{6,5},{7,6},{8,7},{9,8},{10,9... | collective-permute-start | bytes 6152 | tf_op jit(solution)/shard_map/ppermute | solution.py:21
  345.1 13.1 %collective-permute-start.41 = (f32[32,16]{0,1:T(8,128)S(1)}, f32[32,16]{0,1:T(8,128)S(1)}, u32[]{:S(2)}, u32[]{:S(2)}) collective-permute-start(f32[32,16]{0,1:T(8,128)S(1)} %collective-permute-done.40), channel_id=1, source_target_pairs={{0,1},{1,2},{2,3},{3,4},{4,5},{5,6},{6,7},{7,8},{8,9},{9,10},{10,1... | collective-permute-start | bytes 6152 | tf_op jit(solution)/shard_map/ppermute | solution.py:19
  353.8 4.7 collective-permute-start.50
  462.3 3.1 collective-permute-start.51
  462.4 3.1 collective-permute-start.59
  465.5 3.1 collective-permute-start.60
  468.6 4.0 collective-permute-start.61
  472.6 4.0 collective-permute-start.62
  476.6 4.0 collective-permute-start.63
  477.8 3.6 collective-permute-start.56
  480.6 5.4 collective-permute-start.64
  481.4 4.6 collective-permute-start.57
  484.6 5.5 collective-permute-start.66
  486.0 13.0 %collective-permute-start.65 = (f32[32,16]{0,1:T(8,128)S(1)}, f32[32,16]{0,1:T(8,128)S(1)}, u32[]{:S(2)}, u32[]{:S(2)}) collective-permute-start(f32[32,16]{0,1:T(8,128)S(1)} %collective-permute-done.64), channel_id=1, source_target_pairs={{0,15},{1,0},{2,1},{3,2},{4,3},{5,4},{6,5},{7,6},{8,7},{9,8},{10,9... | collective-permute-start | bytes 6152 | tf_op jit(solution)/shard_map/ppermute | solution.py:21
  486.0 13.1 %collective-permute-start.58 = (f32[32,16]{0,1:T(8,128)S(1)}, f32[32,16]{0,1:T(8,128)S(1)}, u32[]{:S(2)}, u32[]{:S(2)}) collective-permute-start(f32[32,16]{0,1:T(8,128)S(1)} %collective-permute-done.57), channel_id=1, source_target_pairs={{0,1},{1,2},{2,3},{3,4},{4,5},{5,6},{6,7},{7,8},{8,9},{9,10},{10,1... | collective-permute-start | bytes 6152 | tf_op jit(solution)/shard_map/ppermute | solution.py:19
  494.7 4.7 collective-permute-start.67
  (10 other events, 66.9 us)
Sparse Core Ops, SparseCore 0:
  20.5 97.5 all-reduce.2
  121.6 54.9 reduce-scatter.1
